TPU v7x, 32 devices: a whole 2x2x4 slice. The times are simulated.
32 devices in a mesh: grp: 2 (over x), seq: 16 (over z, y, core).
Axes of the slice: x: 2, y: 2, z: 4, core: 2. Of those that a mesh axis runs over, the one named last changes fastest.
Arguments:
- tokens: bfloat16 [16384, 1024], P(('grp', 'seq')), parts along dimension 0, may hold values from -6 to 6
- value_weight: bfloat16 [1024, 1024], replicated, may hold values from -0.1875 to 0.1875
- gate_weight: bfloat16 [1024, 1024], replicated, may hold values from -0.1875 to 0.1875
- out_weight: bfloat16 [1024, 1024], replicated, may hold values from -0.1875 to 0.1875
- kernel_weight: bfloat16 [1024, 16], replicated, may hold values from -0.1875 to 0.1875
- kernel_bias: float32 [16], replicated, may hold values from -4 to 4
Outputs:
- mixed: bfloat16 [16384, 1024], P(('grp', 'seq')), parts along dimension 0
There are 2 independent parts, one for each index of `grp`. A program takes and returns all parts, laid end to end along the dimension named above; an argument that names none is the same for every part. Nothing has to cross between parts.
All inputs are finite; a program needn't handle non-finite values.
Results may differ from a plain program's by a relative error of at most 0.0071.
Values may be sent and summed in bfloat16 or wider, within the bound.
A program may use at most 128 MiB of HBM per device.

v0:
```python
import functools

import jax
import jax.numpy as jnp
from jax import lax
from jax.experimental import pallas as pl
from jax.experimental.pallas import tpu as pltpu
from jax.sharding import PartitionSpec as P

MESH = pl.DeviceIdType.MESH


def convolve_kernel(n, values_ref, lag_ref, out_ref, held, lags, band, result, sems):
    width, rows = values_ref.shape[1:]
    length = n * rows
    me = lax.axis_index("seq")
    barrier = pltpu.get_barrier_semaphore()

    def greet(step, carry):
        pl.semaphore_signal(barrier, inc=1, device_id={"seq": lax.rem(me + step, n)}, device_id_type=MESH)
        return carry

    lax.fori_loop(1, n, greet, 0)
    pl.semaphore_wait(barrier, n - 1)

    def copy(kind, source, target, step, peer):
        return pltpu.make_async_remote_copy(
            src_ref=source,
            dst_ref=target,
            send_sem=sems.at[2 * kind, step],
            recv_sem=sems.at[2 * kind + 1, step],
            device_id={"seq": peer},
            device_id_type=MESH,
        )

    def lag_copy(step):
        peer = lax.rem(me + step, n)
        return copy(0, lag_ref.at[peer], lags.at[me], step, peer)

    def value_copy(step):
        peer = lax.rem(me + step, n)
        return copy(1, values_ref.at[peer], held.at[me], step, peer)

    def back_copy(step):
        peer = lax.rem(me + step, n)
        return copy(2, result.at[peer], out_ref.at[me], step, peer)

    def loop(action):
        def run(step, carry):
            action(step)
            return carry

        lax.fori_loop(1, n, run, 0)

    loop(lambda step: lag_copy(step).start())
    loop(lambda step: value_copy(step).start())
    lags[me] = lag_ref[me]
    held[me] = values_ref[me]
    loop(lambda step: lag_copy(step).wait())
    half = 128
    row = jnp.concatenate([lags[place] for place in range(n)], axis=1)
    row = jnp.concatenate([row[:, length - rows - half :], row], axis=1)
    tile = 512
    for start in range(0, length + rows, tile):
        size = min(tile, length + rows - start)
        piece = jnp.broadcast_to(row[:, start : start + size + half], (half, size + half))
        turned = pltpu.roll(piece, 0, 1, stride=1, stride_axis=0)[:, half:].astype(jnp.bfloat16)
        band[:, start : start + size] = turned
    loop(lambda step: value_copy(step).wait())
    held[n : 2 * n] = held[0:n]

    group = max(1, 256 // width)
    reach = min(n, 16)

    def outputs(index, carry):
        first = index * group
        total = None
        for base in range(0, n, reach):
            left = jnp.concatenate(
                [held[pl.ds(first + place, group)].reshape(group * width, rows) for place in range(base, base + reach)],
                axis=1,
            )
            right = jnp.concatenate(
                [
                    band[:, pl.ds((rows - at) if at <= rows else length + rows - at, rows)]
                    for at in range(base * rows, (base + reach) * rows, half)
                ],
                axis=0,
            )
            term = jnp.dot(left, right, preferred_element_type=jnp.float32)
            total = term if total is None else total + term
        result[pl.ds(first, group)] = total.astype(jnp.bfloat16).reshape(group, width, rows)
        return carry

    lax.fori_loop(0, n // group, outputs, 0)
    loop(lambda step: back_copy(step).start())
    out_ref[me] = result[me]
    loop(lambda step: back_copy(step).wait())


def body(tokens, value_weight, gate_weight, out_weight, kernel_weight, kernel_bias):
    rows, model_width = tokens.shape
    heads = kernel_weight.shape[1]
    n = lax.axis_size("seq")
    width = model_width // n
    length = rows * n
    contract = (((0,), (1,)), ((), ()))
    values_t = lax.dot_general(
        value_weight, tokens, contract, preferred_element_type=jnp.float32
    ).astype(jnp.bfloat16)
    gate_t = lax.dot_general(gate_weight, tokens, contract, preferred_element_type=jnp.float32)
    logits = (
        lax.dot_general(kernel_weight, tokens, contract, preferred_element_type=jnp.float32)
        + kernel_bias[:, None]
    )
    lags = (jnp.tanh(logits) * length ** (-0.5)).astype(jnp.bfloat16).astype(jnp.float32)
    lags = jnp.repeat(lags, n // heads, axis=0).reshape(n, 1, rows)
    vmem = pl.BlockSpec(memory_space=pltpu.VMEM)
    conv_t = pl.pallas_call(
        functools.partial(convolve_kernel, n),
        out_shape=jax.ShapeDtypeStruct((n, width, rows), jnp.bfloat16),
        in_specs=[vmem, vmem],
        out_specs=vmem,
        scratch_shapes=[
            pltpu.VMEM((2 * n, width, rows), jnp.bfloat16),
            pltpu.VMEM((n, 1, rows), jnp.float32),
            pltpu.VMEM((128, length + rows), jnp.bfloat16),
            pltpu.VMEM((n, width, rows), jnp.bfloat16),
            pltpu.SemaphoreType.DMA((6, n)),
        ],
        compiler_params=pltpu.CompilerParams(
            collective_id=0, has_side_effects=True, vmem_limit_bytes=60 * 2**20
        ),
    )(values_t.reshape(n, width, rows), lags)
    conv_t = conv_t.reshape(model_width, rows)
    gated_t = (conv_t.astype(jnp.float32) * jax.nn.silu(gate_t)).astype(jnp.bfloat16)
    mixed = lax.dot_general(
        gated_t, out_weight, (((0,), (0,)), ((), ())), preferred_element_type=jnp.float32
    )
    return mixed.astype(jnp.bfloat16)


def solution(mesh):
    placed = (P(("grp", "seq"), None), P(), P(), P(), P(), P())
    return jax.shard_map(
        body, mesh=mesh, in_specs=placed, out_specs=P(("grp", "seq"), None), check_vma=False
    )
```

profile of v0, /device:TPU:31, one launch (start us, length us, event | category | flops | bytes accessed | tf_op | source)
XLA Modules:
  0.0 75.7 jit_solution(18297533825286393277)
XLA Ops:
  0.0 0.0 copy-start
  0.0 1.8 %fusion.4 = f32[16,512]{1,0:T(8,128)S(1)} fusion(bf16[1024,16]{0,1:T(8,128)(2,1)} %param.10, bf16[512,1024]{1,0:T(8,128)(2,1)} %param.6, f32[16]{0:T(128)} %param.11), kind=kOutput, calls=%fused_computation.8 | convolution fusion | flops 16809984 | bytes 1114176 | tf_op jit(solution)/shard_map/dot_general | solution.py:113
  1.8 0.6 reshape.8.lag_ref
  2.4 0.0 copy-done
  2.4 3.5 %convolution_convert_fusion.1 = bf16[1024,512]{1,0:T(8,128)(2,1)} fusion(bf16[1024,1024]{1,0:T(8,128)(2,1)S(1)} %copy-done, bf16[512,1024]{1,0:T(8,128)(2,1)} %param.6), kind=kOutput, calls=%fused_computation.3 | convolution fusion | flops 1074266112 | bytes 4194304 | tf_op jit(solution)/shard_map/dot_general | solution.py:108
  5.9 0.0 copy-start.2
  5.9 63.9 %shard_map.64 = bf16[16,64,512]{2,1,0:T(8,128)(2,1)} custom-call(bf16[16,64,512]{2,1,0:T(8,128)(2,1)} %bitcast.12, f32[16,1,512]{2,1,0:T(1,128)} %reshape.8.lag_ref), custom_call_target="tpu_custom_call" | custom-call | tf_op jit(solution)/shard_map/pallas_call | solution.py:119
  69.8 0.0 copy-done.2
  69.8 0.0 copy-start.1
  69.8 3.6 %fusion = bf16[1024,512]{1,0:T(8,128)(2,1)S(1)} fusion(bf16[16,64,512]{2,1,0:T(8,128)(2,1)} %shard_map.64, bf16[1024,1024]{1,0:T(8,128)(2,1)} %param.8, bf16[512,1024]{1,0:T(8,128)(2,1)S(1)} %copy-done.2), kind=kOutput, calls=%fused_computation.1 | convolution fusion | flops 1077411840 | bytes 5242880 | tf_op jit(solution)/shard_map/dot_general | solution.py:111
  73.5 0.0 copy-done.1
  73.5 2.2 %convolution_convert_fusion = bf16[512,1024]{1,0:T(8,128)(2,1)} fusion(bf16[1024,512]{1,0:T(8,128)(2,1)S(1)} %fusion, bf16[1024,1024]{1,0:T(8,128)(2,1)S(1)} %copy-done.1), kind=kOutput, calls=%fused_computation.2 | convolution fusion | flops 1074266112 | bytes 4194304 | tf_op jit(solution)/shard_map/dot_general | solution.py:137
Async XLA Ops:
  0.0 2.4 %copy-start = (bf16[1024,1024]{1,0:T(8,128)(2,1)S(1)}, bf16[1024,1024]{1,0:T(8,128)(2,1)}, u32[]{:S(2)}) copy-start(bf16[1024,1024]{1,0:T(8,128)(2,1)} %param.7) | copy-start | bytes 6291460
  5.9 63.9 %copy-start.2 = (bf16[512,1024]{1,0:T(8,128)(2,1)S(1)}, bf16[512,1024]{1,0:T(8,128)(2,1)}, u32[]{:S(2)}) copy-start(bf16[512,1024]{1,0:T(8,128)(2,1)} %param.6) | copy-start | bytes 3145732
  69.8 3.7 %copy-start.1 = (bf16[1024,1024]{1,0:T(8,128)(2,1)S(1)}, bf16[1024,1024]{1,0:T(8,128)(2,1)}, u32[]{:S(2)}) copy-start(bf16[1024,1024]{1,0:T(8,128)(2,1)} %param.9) | copy-start | bytes 6291460
where the time goes:
time: 75.9 us; the launch traced here: 75.7 us
  Pallas kernels  63.9 us (84%)
  matrix products  11.1 us (15%)
    pallas_call x1, Pallas kernels, body(): pl.pallas_call(functools.partial(convolve_kernel, n), out_shape=jax.Shape...  63.9 us
    dot_general x1, matrix products, body(): lax.dot_general(gate_weight, tokens, contract, preferred_element_type=jnp...  3.65 us
    dot_general x1, matrix products, body(): lax.dot_general(value_weight, tokens, contract, preferred_element_type=jn...  3.49 us
    dot_general x1, matrix products, body(): lax.dot_general(gated_t, out_weight, (((0,), (0,)), ((), ())), preferred_...  2.24 us
    dot_general x1, matrix products, body(): lax.dot_general(kernel_weight, tokens, contract, preferred_element_type=j...  1.77 us

commit v1 on v0

v1 whole, which is shorter than its diff:
```python
import functools

import jax
import jax.numpy as jnp
from jax import lax
from jax.experimental import pallas as pl
from jax.experimental.pallas import tpu as pltpu
from jax.sharding import PartitionSpec as P

MESH = pl.DeviceIdType.MESH
LANES = 128
BLOCK = 256
CHUNKS = 4


def layer_kernel(
    n,
    heads,
    tokens_hbm,
    value_hbm,
    gate_hbm,
    out_hbm,
    head_ref,
    bias_ref,
    mixed_ref,
    tokens,
    value_w,
    gate_w,
    out_w,
    outgoing,
    held,
    lag_send,
    lags,
    band,
    open_gate,
    result,
    returned,
    total,
    load_sems,
    lag_sems,
    sems,
):
    rows, model = tokens.shape
    chunks, _, wide, _ = outgoing.shape
    width = chunks * wide
    length = n * rows
    per = BLOCK // width
    blocks = n // per
    share = n // heads
    me = lax.axis_index("seq")
    mine = me // per
    order = sorted(range(blocks), key=lambda off: (-min(off, blocks - off), off))

    def place(off):
        return lax.rem(mine + off, blocks)

    def load(source, target, slot):
        return pltpu.make_async_copy(source, target, load_sems.at[slot])

    def value_load(off):
        columns = pl.ds(pl.multiple_of(place(off) * BLOCK, BLOCK), BLOCK)
        return load(value_hbm.at[:, columns], value_w.at[off], 3 + off)

    tokens_load = load(tokens_hbm, tokens, 0)
    gate_load = load(gate_hbm, gate_w, 1)
    out_load = load(out_hbm, out_w, 2)
    tokens_load.start()
    for off in order:
        value_load(off).start()
    gate_load.start()
    out_load.start()

    barrier = pltpu.get_barrier_semaphore()

    def loop(action):
        def run(step, carry):
            action(step)
            return carry

        lax.fori_loop(1, n, run, 0)

    loop(
        lambda step: pl.semaphore_signal(
            barrier, inc=1, device_id={"seq": lax.rem(me + step, n)}, device_id_type=MESH
        )
    )

    def lag_copy(step):
        peer = lax.rem(me + step, n)
        return pltpu.make_async_remote_copy(
            src_ref=lag_send.at[peer // share],
            dst_ref=lags.at[me],
            send_sem=lag_sems.at[0, step],
            recv_sem=lag_sems.at[1, step],
            device_id={"seq": peer},
            device_id_type=MESH,
        )

    def remote(kind, source, target, chunk, step):
        peer = lax.rem(me + step, n)
        return pltpu.make_async_remote_copy(
            src_ref=source.at[chunk, peer],
            dst_ref=target.at[chunk, me],
            send_sem=sems.at[2 * kind, chunk, step],
            recv_sem=sems.at[2 * kind + 1, chunk, step],
            device_id={"seq": peer},
            device_id_type=MESH,
        )

    def value_copy(chunk, step):
        return remote(0, outgoing, held, chunk, step)

    def back_copy(chunk, step):
        return remote(1, result, returned, chunk, step)

    def send_block(off, chunk, make):
        inside = lax.rem(me, per)
        for turn in range(1 if off == 0 else 0, per):
            peer = place(off) * per + lax.rem(inside + turn, per)
            make(chunk, lax.rem(peer - me + n, n)).start()

    tokens_load.wait()
    logits = jnp.dot(tokens[...], head_ref[...], preferred_element_type=jnp.float32) + bias_ref[...]
    made = (jnp.tanh(logits) * length ** (-0.5)).astype(jnp.bfloat16).astype(jnp.float32).T
    for head in range(heads):
        lag_send[head] = made[head : head + 1]
    pl.semaphore_wait(barrier, n - 1)
    loop(lambda step: lag_copy(step).start())
    lags[me] = lag_send[me // share]

    for off in order:
        value_load(off).wait()
        block = jnp.dot(tokens[...], value_w[off], preferred_element_type=jnp.float32)
        block = block.astype(jnp.bfloat16).T.reshape(per, chunks, wide, rows)
        for chunk in range(chunks):
            outgoing[chunk, pl.ds(place(off) * per, per)] = block[:, chunk]
        send_block(off, 0, value_copy)
    for chunk in range(1, chunks):
        for off in order:
            send_block(off, chunk, value_copy)
    for chunk in range(chunks):
        held[chunk, me] = outgoing[chunk, me]

    loop(lambda step: lag_copy(step).wait())
    row = jnp.concatenate([lags[source] for source in range(n)], axis=1)
    row = jnp.concatenate([row[:, length - rows - LANES :], row], axis=1)
    for start in range(0, length + rows, rows):
        piece = jnp.broadcast_to(row[:, start : start + rows + LANES], (LANES, rows + LANES))
        turned = pltpu.roll(piece, 0, 1, stride=1, stride_axis=0)[:, LANES:]
        band[:, start : start + rows] = turned.astype(jnp.bfloat16)

    gate_load.wait()
    for part in range(model // BLOCK):
        gate = jnp.dot(
            tokens[...], gate_w[:, part * BLOCK : (part + 1) * BLOCK], preferred_element_type=jnp.float32
        )
        gate = (gate / (1.0 + jnp.exp(-gate))).T.reshape(per, chunks, wide, rows)
        for chunk in range(chunks):
            open_gate[chunk, part * per : (part + 1) * per] = gate[:, chunk]

    group = min(n, max(1, BLOCK // wide))
    reach = min(n, 16)

    def convolve(chunk, carry):
        loop(lambda step: value_copy(chunk, step).wait())
        held[chunk, n : 2 * n] = held[chunk, 0:n]

        def outputs(index, inner):
            first = index * group
            summed = None
            for base in range(0, n, reach):
                left = jnp.concatenate(
                    [
                        held[chunk, pl.ds(first + at, group)].reshape(group * wide, rows)
                        for at in range(base, base + reach)
                    ],
                    axis=1,
                )
                right = jnp.concatenate(
                    [
                        band[:, pl.ds((rows - at) if at <= rows else length + rows - at, rows)]
                        for at in range(base * rows, (base + reach) * rows, LANES)
                    ],
                    axis=0,
                )
                term = jnp.dot(left, right, preferred_element_type=jnp.float32)
                summed = term if summed is None else summed + term
            result[chunk, pl.ds(first, group)] = summed.astype(jnp.bfloat16).reshape(group, wide, rows)
            return inner

        lax.fori_loop(0, n // group, outputs, 0)
        for off in order:
            send_block(off, chunk, back_copy)
        returned[chunk, me] = result[chunk, me]
        return carry

    lax.fori_loop(0, chunks, convolve, 0)

    out_load.wait()
    for chunk in range(chunks):
        loop(lambda step: back_copy(chunk, step).wait())
        gated = (returned[chunk].astype(jnp.float32) * open_gate[chunk]).astype(jnp.bfloat16)
        weight = out_w[:, chunk].reshape(n * wide, model)
        term = jnp.dot(gated.reshape(n * wide, rows).T, weight, preferred_element_type=jnp.float32)
        if chunk > 0:
            term = total[...] + term
        if chunk < chunks - 1:
            total[...] = term
        else:
            mixed_ref[...] = term.astype(jnp.bfloat16)


def body(tokens, value_weight, gate_weight, out_weight, kernel_weight, kernel_bias):
    rows, model = tokens.shape
    heads = kernel_weight.shape[1]
    n = lax.axis_size("seq")
    width = model // n
    chunks = max(1, min(CHUNKS, width // 16))
    wide = width // chunks
    length = rows * n
    per = BLOCK // width
    vmem = pl.BlockSpec(memory_space=pltpu.VMEM)
    anywhere = pl.BlockSpec(memory_space=pl.ANY)
    half = jnp.bfloat16
    return pl.pallas_call(
        functools.partial(layer_kernel, n, heads),
        out_shape=jax.ShapeDtypeStruct((rows, model), half),
        in_specs=[anywhere] * 4 + [vmem] * 2,
        out_specs=vmem,
        scratch_shapes=[
            pltpu.VMEM((rows, model), half),
            pltpu.VMEM((n // per, model, BLOCK), half),
            pltpu.VMEM((model, model), half),
            pltpu.VMEM((n, chunks, wide, model), half),
            pltpu.VMEM((chunks, n, wide, rows), half),
            pltpu.VMEM((chunks, 2 * n, wide, rows), half),
            pltpu.VMEM((heads, 1, rows), jnp.float32),
            pltpu.VMEM((n, 1, rows), jnp.float32),
            pltpu.VMEM((LANES, length + rows), half),
            pltpu.VMEM((chunks, n, wide, rows), jnp.float32),
            pltpu.VMEM((chunks, n, wide, rows), half),
            pltpu.VMEM((chunks, n, wide, rows), half),
            pltpu.VMEM((rows, model), jnp.float32),
            pltpu.SemaphoreType.DMA((3 + n // per,)),
            pltpu.SemaphoreType.DMA((2, n)),
            pltpu.SemaphoreType.DMA((4, chunks, n)),
        ],
        compiler_params=pltpu.CompilerParams(
            collective_id=0, has_side_effects=True, vmem_limit_bytes=60 * 2**20
        ),
    )(
        tokens,
        value_weight,
        gate_weight,
        out_weight.reshape(n, chunks, wide, model),
        kernel_weight,
        kernel_bias.reshape(1, heads),
    )


def solution(mesh):
    placed = (P(("grp", "seq"), None), P(), P(), P(), P(), P())
    return jax.shard_map(
        body, mesh=mesh, in_specs=placed, out_specs=P(("grp", "seq"), None), check_vma=False
    )
```

time: 75.9 us -> 61.8 us (0.81)
  the two profiles are of different devices: /device:TPU:31 before, /device:TPU:0 now
where the time goes in v1:
time: 61.8 us; the launch traced here: 61.5 us
  Pallas kernels  57.7 us (93%)
  local copies, waits for them, and re-layouts  3.86 us (6%)
    pallas_call x1, Pallas kernels, body(): pl.pallas_call(functools.partial(layer_kernel, n, heads), out_shape=jax.S...  57.7 us
    unnamed x2, local copies, waits for them, and re-layouts  3.86 us

profile of v1, /device:TPU:0, one launch (start us, length us, event | category | flops | bytes accessed | tf_op | source)
XLA Modules:
  0.0 61.5 jit_solution(8386150434265673304)
XLA Ops:
  0.0 1.6 %copy.7.head_ref = bf16[1024,16]{1,0:T(8,128)(2,1)} copy(bf16[1024,16]{0,1:T(8,128)(2,1)} %param.10) | data formatting | bytes 65536 | tf_op args[4]
  1.6 57.7 %shard_map.64 = bf16[512,1024]{1,0:T(8,128)(2,1)} custom-call(bf16[512,1024]{1,0:T(8,128)(2,1)} %tokens_hbm.1, bf16[1024,1024]{1,0:T(8,128)(2,1)} %value_hbm.1, bf16[1024,1024]{1,0:T(8,128)(2,1)} %gate_hbm.1, bf16[16,4,16,1024]{3,2,1,0:T(8,128)(2,1)} %bitcast.2, bf16[1024,16]{1,0:T(8,128)(2,1)} %copy.7.head_ref, f32[1,16]{1,0:T(1,128)} %bitcast.3), custom_call_target="tpu_custom_call" | custom-call | tf_op jit(solution)/shard_map/pallas_call | solution.py:225
  59.3 2.3 %copy.9 = bf16[512,1024]{1,0:T(8,128)(2,1)} copy(bf16[512,1024]{1,0:T(8,128)(2,1)} %shard_map.64) | data formatting | bytes 2097152

commit v2 on v1

--- a/solution.py
+++ b/solution.py
@@ -10,7 +10,7 @@
 MESH = pl.DeviceIdType.MESH
 LANES = 128
 BLOCK = 256
-CHUNKS = 4
+CHUNKS = 2
 
 
 def layer_kernel(
@@ -49,10 +49,14 @@
     share = n // heads
     me = lax.axis_index("seq")
     mine = me // per
-    order = sorted(range(blocks), key=lambda off: (-min(off, blocks - off), off))
+    side = blocks // 2
+    order = range(blocks)
 
     def place(off):
-        return lax.rem(mine + off, blocks)
+        near = mine // side
+        if off < side:
+            return (1 - near) * side + lax.rem(mine + off, side)
+        return near * side + lax.rem(mine + off + 1, side)
 
     def load(source, target, slot):
         return pltpu.make_async_copy(source, target, load_sems.at[slot])
@@ -64,12 +68,6 @@
     tokens_load = load(tokens_hbm, tokens, 0)
     gate_load = load(gate_hbm, gate_w, 1)
     out_load = load(out_hbm, out_w, 2)
-    tokens_load.start()
-    for off in order:
-        value_load(off).start()
-    gate_load.start()
-    out_load.start()
-
     barrier = pltpu.get_barrier_semaphore()
 
     def loop(action):
@@ -84,6 +82,10 @@
             barrier, inc=1, device_id={"seq": lax.rem(me + step, n)}, device_id_type=MESH
         )
     )
+
+    tokens_load.start()
+    for off in order:
+        value_load(off).start()
 
     def lag_copy(step):
         peer = lax.rem(me + step, n)
@@ -115,26 +117,31 @@
 
     def send_block(off, chunk, make):
         inside = lax.rem(me, per)
-        for turn in range(1 if off == 0 else 0, per):
+        for turn in range(1 if off == blocks - 1 else 0, per):
             peer = place(off) * per + lax.rem(inside + turn, per)
             make(chunk, lax.rem(peer - me + n, n)).start()
 
     tokens_load.wait()
-    logits = jnp.dot(tokens[...], head_ref[...], preferred_element_type=jnp.float32) + bias_ref[...]
-    made = (jnp.tanh(logits) * length ** (-0.5)).astype(jnp.bfloat16).astype(jnp.float32).T
-    for head in range(heads):
-        lag_send[head] = made[head : head + 1]
-    pl.semaphore_wait(barrier, n - 1)
-    loop(lambda step: lag_copy(step).start())
-    lags[me] = lag_send[me // share]
-
     for off in order:
         value_load(off).wait()
         block = jnp.dot(tokens[...], value_w[off], preferred_element_type=jnp.float32)
         block = block.astype(jnp.bfloat16).T.reshape(per, chunks, wide, rows)
         for chunk in range(chunks):
             outgoing[chunk, pl.ds(place(off) * per, per)] = block[:, chunk]
+        if off == 0:
+            pl.semaphore_wait(barrier, n - 1)
         send_block(off, 0, value_copy)
+        if off == 0:
+            gate_load.start()
+            out_load.start()
+            logits = lax.dot_general(
+                head_ref[...], tokens[...], (((1,), (1,)), ((), ())), preferred_element_type=jnp.float32
+            )
+            for head in range(heads):
+                made = jnp.tanh(logits[head : head + 1] + bias_ref[0, head]) * length ** (-0.5)
+                lag_send[head] = made.astype(jnp.bfloat16).astype(jnp.float32)
+            loop(lambda step: lag_copy(step).start())
+            lags[me] = lag_send[me // share]
     for chunk in range(1, chunks):
         for off in order:
             send_block(off, chunk, value_copy)
@@ -197,17 +204,34 @@
     lax.fori_loop(0, chunks, convolve, 0)
 
     out_load.wait()
+    part = n // 2
     for chunk in range(chunks):
-        loop(lambda step: back_copy(chunk, step).wait())
-        gated = (returned[chunk].astype(jnp.float32) * open_gate[chunk]).astype(jnp.bfloat16)
-        weight = out_w[:, chunk].reshape(n * wide, model)
-        term = jnp.dot(gated.reshape(n * wide, rows).T, weight, preferred_element_type=jnp.float32)
-        if chunk > 0:
-            term = total[...] + term
-        if chunk < chunks - 1:
-            total[...] = term
-        else:
-            mixed_ref[...] = term.astype(jnp.bfloat16)
+        for far in range(2):
+            base = (me // part) * part if far == 0 else (1 - me // part) * part
+
+            def arrive(index, carry):
+                step = lax.rem(me - (base + index) + n, n)
+
+                @pl.when(step > 0)
+                def _():
+                    back_copy(chunk, step).wait_recv()
+
+                return carry
+
+            lax.fori_loop(0, part, arrive, 0)
+            chosen = pl.ds(base, part)
+            gated = returned[chunk, chosen].astype(jnp.float32) * open_gate[chunk, chosen]
+            gated = gated.astype(jnp.bfloat16).reshape(part * wide, rows).T
+            weight = out_w[chosen, chunk].reshape(part * wide, model)
+            term = jnp.dot(gated, weight, preferred_element_type=jnp.float32)
+            if chunk + far > 0:
+                term = total[...] + term
+            if chunk + far < chunks:
+                total[...] = term
+            else:
+                mixed_ref[...] = term.astype(jnp.bfloat16)
+    for chunk in range(chunks):
+        loop(lambda step: back_copy(chunk, step).wait_send())
 
 
 def body(tokens, value_weight, gate_weight, out_weight, kernel_weight, kernel_bias):
@@ -225,7 +249,7 @@
     return pl.pallas_call(
         functools.partial(layer_kernel, n, heads),
         out_shape=jax.ShapeDtypeStruct((rows, model), half),
-        in_specs=[anywhere] * 4 + [vmem] * 2,
+        in_specs=[anywhere] * 4 + [vmem, pl.BlockSpec(memory_space=pltpu.SMEM)],
         out_specs=vmem,
         scratch_shapes=[
             pltpu.VMEM((rows, model), half),
@@ -253,7 +277,7 @@
         value_weight,
         gate_weight,
         out_weight.reshape(n, chunks, wide, model),
-        kernel_weight,
+        kernel_weight.T,
         kernel_bias.reshape(1, heads),
     )
 

time: 61.8 us -> 60.1 us (0.972)
  local copies, waits for them, and re-layouts: 3.86 us -> 2.26 us
    unnamed x2 -> x1, local copies, waits for them, and re-layouts: 3.86 us -> 2.26 us
where the time goes in v2:
time: 60.1 us; the launch traced here: 59.9 us
  Pallas kernels  57.6 us (96%)
  local copies, waits for them, and re-layouts  2.26 us (4%)
    pallas_call x1, Pallas kernels, body(): pl.pallas_call(functools.partial(layer_kernel, n, heads), out_shape=jax.S...  57.6 us
    unnamed x1, local copies, waits for them, and re-layouts  2.26 us

profile of v2, /device:TPU:0, one launch (start us, length us, event | category | flops | bytes accessed | tf_op | source)
XLA Modules:
  0.0 59.9 jit_solution(899566912545664224)
XLA Ops:
  0.0 57.6 %shard_map.64 = bf16[512,1024]{1,0:T(8,128)(2,1)} custom-call(bf16[512,1024]{1,0:T(8,128)(2,1)} %tokens_hbm.1, bf16[1024,1024]{1,0:T(8,128)(2,1)} %value_hbm.1, bf16[1024,1024]{1,0:T(8,128)(2,1)} %gate_hbm.1, bf16[16,2,32,1024]{3,2,1,0:T(8,128)(2,1)} %bitcast.3, bf16[16,1024]{1,0:T(8,128)(2,1)} %bitcast.4, f32[1,16]{1,0:T(1,128)} %bitcast.5), custom_call_target="tpu_custom_call" | custom-call | tf_op jit(solution)/shard_map/pallas_call | solution.py:249
  57.6 2.3 %copy.8 = bf16[512,1024]{1,0:T(8,128)(2,1)} copy(bf16[512,1024]{1,0:T(8,128)(2,1)} %shard_map.64) | data formatting | bytes 2097152

commit v3 on v2

--- a/solution.py
+++ b/solution.py
@@ -49,14 +49,11 @@
     share = n // heads
     me = lax.axis_index("seq")
     mine = me // per
-    side = blocks // 2
+    distance = sorted(range(blocks), key=lambda off: (-min(off, blocks - off), off))
     order = range(blocks)
 
     def place(off):
-        near = mine // side
-        if off < side:
-            return (1 - near) * side + lax.rem(mine + off, side)
-        return near * side + lax.rem(mine + off + 1, side)
+        return lax.rem(mine + distance[off], blocks)
 
     def load(source, target, slot):
         return pltpu.make_async_copy(source, target, load_sems.at[slot])

time: 60.1 us -> 57.5 us (0.957)
  Pallas kernels: 57.6 us -> 54.9 us
    pallas_call x1, Pallas kernels: 57.6 us -> 54.9 us  [body(): pl.pallas_call(functools.partial(layer_kernel, n, heads), out_shape=jax.S...]
where the time goes in v3:
time: 57.5 us; the launch traced here: 57.2 us
  Pallas kernels  54.9 us (95%)
  local copies, waits for them, and re-layouts  2.26 us (4%)
    pallas_call x1, Pallas kernels, body(): pl.pallas_call(functools.partial(layer_kernel, n, heads), out_shape=jax.S...  54.9 us
    unnamed x1, local copies, waits for them, and re-layouts  2.26 us

profile of v3, /device:TPU:0, one launch (start us, length us, event | category | flops | bytes accessed | tf_op | source)
XLA Modules:
  0.0 57.2 jit_solution(11346385593129777345)
XLA Ops:
  0.0 54.9 %shard_map.64 = bf16[512,1024]{1,0:T(8,128)(2,1)} custom-call(bf16[512,1024]{1,0:T(8,128)(2,1)} %tokens_hbm.1, bf16[1024,1024]{1,0:T(8,128)(2,1)} %value_hbm.1, bf16[1024,1024]{1,0:T(8,128)(2,1)} %gate_hbm.1, bf16[16,2,32,1024]{3,2,1,0:T(8,128)(2,1)} %bitcast.3, bf16[16,1024]{1,0:T(8,128)(2,1)} %bitcast.4, f32[1,16]{1,0:T(1,128)} %bitcast.5), custom_call_target="tpu_custom_call" | custom-call | tf_op jit(solution)/shard_map/pallas_call | solution.py:246
  54.9 2.3 %copy.8 = bf16[512,1024]{1,0:T(8,128)(2,1)} copy(bf16[512,1024]{1,0:T(8,128)(2,1)} %shard_map.64) | data formatting | bytes 2097152
